TPU v7x, 32 devices: a whole 2x2x4 slice. The times are simulated.
32 devices in a mesh: ch: 8 (over y, x, core), grp: 4 (over z).
Axes of the slice: x: 2, y: 2, z: 4, core: 2. Of those that a mesh axis runs over, the one named last changes fastest.
Arguments:
- raw: float32 [512, 4096], P(('ch', 'grp')), may hold values from -128 to 128, as said below
- fir_taps: float32 [129], replicated, may hold values from -4 to 4
- chan_map: int32 [4096], replicated, may hold values from 0 to 4095, each once
- order: int32 [3], replicated, may hold values from 0 to 31, as said below
Outputs:
- correlations: float32 [3, 32, 257, 4096], P(None, None, None, ('ch', 'grp'))
Inputs may be any that keep to these rules, and one draw needn't show every extreme that they name: `order`: 3 distinct device indices; the device with flat index i over ch and grp holds regrouped channels i * 128 to (i + 1) * 128 - 1. `raw`: each time sample and each channel has its own scale.
All inputs are finite; a program needn't handle non-finite values.
Results may differ from a plain program's by a relative error of at most 0.0028.
Values may be sent and summed in bfloat16 or wider, within the bound.
No kernel may reach another device: no remote copies, remote signals or barrier semaphores. Data moves between devices by JAX's collectives and lax.ppermute only.
A program may use at most 128 MiB of HBM per device.

v0:
```python
import math

import jax
import jax.numpy as jnp
from jax import lax
from jax.sharding import PartitionSpec as P

BLK = 512
FIR_HALF = 64
HALF = 128
SB = 32
STEPS = 3
LAGS = 257


def from_root(block, axis, holder):
    block = jnp.where(lax.axis_index(axis) == holder, block, jnp.zeros_like(block))
    return lax.psum(block, axis)


def shifted_rows(vector, count, length, period):
    lead = vector.shape[:-1]
    padded = jnp.pad(vector, [(0, 0)] * len(lead) + [(0, period - vector.shape[-1])])
    spread = jnp.broadcast_to(padded[..., None, :], lead + (count, period))
    flat = spread.reshape(lead + (count * period,))
    cut = flat[..., : count * (period - 1)].reshape(lead + (count, period - 1))
    return cut[..., :length]


def local(raw, fir_taps, chan_map, order):
    columns = jnp.take(raw, chan_map, axis=1)
    mixed = lax.all_to_all(columns, ("ch", "grp"), split_axis=1, concat_axis=0, tiled=True)
    samples, width = mixed.shape
    nblocks = samples // BLK
    starts = jnp.arange(nblocks, dtype=jnp.int32) * BLK
    band = shifted_rows(fir_taps, BLK, BLK + 2 * FIR_HALF, 2 * BLK + 2 * FIR_HALF)
    padded = jnp.pad(mixed, ((FIR_HALF, FIR_HALF), (0, 0)))

    def filter_block(start):
        window = lax.dynamic_slice_in_dim(padded, start, BLK + 2 * FIR_HALF, 0)
        return jnp.dot(band, window, precision=lax.Precision.HIGHEST)

    filtered = lax.map(filter_block, starts).reshape(samples, width)
    power = jnp.mean(filtered * filtered, axis=0)
    whitened = (filtered / jnp.sqrt(power + 1e-06)).astype(jnp.bfloat16)
    own_block = whitened[:, :SB].T
    receivers = jnp.pad(whitened, ((HALF, HALF), (0, 0)))
    results = []
    for step in range(STEPS):
        source = from_root(own_block, ("ch", "grp"), order[step])

        def add_block(total, start):
            piece = lax.dynamic_slice_in_dim(source, start, BLK, 1)
            hankel = shifted_rows(piece, LAGS, BLK + 2 * HALF, BLK + 2 * HALF + 1)
            window = lax.dynamic_slice_in_dim(receivers, start, BLK + 2 * HALF, 0)
            return (
                total
                + jnp.einsum("alj,jr->alr", hankel, window, preferred_element_type=jnp.float32),
                None,
            )

        total, unused = lax.scan(add_block, jnp.zeros((SB, LAGS, width), jnp.float32), starts)
        results.append(total / math.sqrt(samples))
    stacked = jnp.stack(results)
    return stacked


def solution(mesh):
    in_specs = (P(("ch", "grp"), None), P(), P(), P())
    out_specs = P(None, None, None, ("ch", "grp"))
    return jax.shard_map(local, mesh=mesh, in_specs=in_specs, out_specs=out_specs, check_vma=False)
```

profile of v0, /device:TPU:0, one launch (start us, length us, event | category | flops | bytes accessed | tf_op | source)
XLA Modules:
  0.0 358.1 jit_solution(10664348099747867866)
XLA Ops:
  6.5 0.7 and_bitcast_fusion
  7.3 0.7 fusion.9
  8.0 1.5 copy.10
  9.5 14.2 %gather_fusion = f32[4096,16]{1,0:T(8,128)} fusion(f32[16,4096]{0,1:T(8,128)S(1)} %copy.10, s32[4096]{0:T(1024)S(1)} %fusion.9), kind=kCustom, calls=%fused_computation | custom fusion | bytes 540672 | tf_op jit(solution)/shard_map/jit(_take)/gather | solution.py:31
  23.7 2.2 copy.11
  25.9 0.7 broadcast_select_fusion
  26.6 7.3 %all-to-all-start = ((f32[16,32,128]{2,0,1:T(8,128)}), f32[16,32,128]{2,0,1:T(8,128)S(1)}, u32[]{:S(2)}, u32[]{:S(2)}) async-start(f32[16,32,128]{2,0,1:T(8,128)} %broadcast_select_fusion), calls=%async_computation | async-start | bytes 524288 | tf_op jit(solution)/shard_map/all_to_all | solution.py:32
  33.9 0.0 all-reduce.9.cloned.1.call-start
  34.0 1.4 fusion.14
  37.2 0.7 pad.25
  37.9 0.2 broadcast_in_dim.55
  38.0 1.6 reshape.55
  39.6 3.6 %reshape.56 = f32[512,1151]{1,0:T(8,128)S(1)} reshape(f32[589312]{0:T(1024)} %bitcast.36) | data formatting | bytes 4714496 | tf_op jit(solution)/shard_map/reshape | solution.py:26
  43.2 0.9 all-to-all-done
  44.1 1.6 multiply_reduce_fusion
  45.7 0.1 divide_convert_fusion
  45.8 0.6 select_bitcast_fusion.2
  46.5 0.0 all-reduce.9.cloned.1.call-update
  46.5 122.3 %all-reduce.9.cloned.1.call-done = (bf16[32,512]{1,0:T(8,128)(2,1)}, bf16[32,512]{1,0:T(8,128)(2,1)}, bf16[32,512]{1,0:T(8,128)(2,1)}) async-done(((bf16[32,512]{1,0:T(8,128)(2,1)}, bf16[32,512]{1,0:T(8,128)(2,1)}, bf16[32,512]{1,0:T(8,128)(2,1)}), (bf16[32,512]{1,0:T(8,128)(2,1)}, bf16[32,512]{1,0:T(8,128)(2,1)}, bf16[32,512]{1,0:T(8,128)(2,1)})) %all-reduce.9.cloned.1.call-update) | async-done | bytes 98320 | tf_op jit(solution)/shard_map/psum | solution.py:18
  168.8 0.8 pad.30
  169.6 0.8 pad.29
  170.4 0.8 pad.27
  171.1 6.4 %broadcast_in_dim.60 = bf16[32,257,769]{2,1,0:T(8,128)(2,1)} broadcast(bf16[32,769]{1,0:T(8,128)(2,1)S(1)} %pad.27), dimensions={0,2} | broadcast | bytes 12697728 | tf_op jit(solution)/shard_map/while/body/eval_jaxpr/broadcast_in_dim | solution.py:24
  177.6 15.3 %reshape.57 = bf16[32,197633]{1,0:T(8,128)(2,1)} reshape(bf16[32,257,769]{2,1,0:T(8,128)(2,1)} %broadcast_in_dim.60) | data formatting | bytes 25297024 | tf_op jit(solution)/shard_map/while/body/eval_jaxpr/reshape | solution.py:25
  192.8 10.5 %slice.44 = bf16[32,197376]{1,0:T(8,128)(2,1)} slice(bf16[32,197633]{1,0:T(8,128)(2,1)} %reshape.57), slice={[0:32], [0:197376]} | slice | bytes 25264128 | tf_op jit(solution)/shard_map/while/body/eval_jaxpr/slice | solution.py:26
  203.3 12.1 %reshape.58 = bf16[32,257,768]{2,1,0:T(8,128)(2,1)} reshape(bf16[32,197376]{1,0:T(8,128)(2,1)} %slice.44) | data formatting | bytes 25264128 | tf_op jit(solution)/shard_map/while/body/eval_jaxpr/reshape | solution.py:26
  215.4 10.3 %multiply_bitcast_fusion.2 = f32[1,32,257,128]{3,2,1,0:T(8,128)} fusion(bf16[32,257,768]{2,1,0:T(8,128)(2,1)} %reshape.58, bf16[512,128]{0,1:T(8,128)(2,1)S(1)} %divide_convert_fusion), kind=kOutput, calls=%fused_computation.4 | convolution fusion | flops 1617956864 | bytes 16973824 | tf_op jit(solution)/shard_map/while/body/eval_jaxpr/alj,jr->alr/dot_general | solution.py:58
  225.7 6.4 %broadcast_in_dim.61 = bf16[32,257,769]{2,1,0:T(8,128)(2,1)} broadcast(bf16[32,769]{1,0:T(8,128)(2,1)S(1)} %pad.29), dimensions={0,2} | broadcast | bytes 12697728 | tf_op jit(solution)/shard_map/while/body/eval_jaxpr/broadcast_in_dim | solution.py:24
  232.1 15.2 %reshape.59 = bf16[32,197633]{1,0:T(8,128)(2,1)} reshape(bf16[32,257,769]{2,1,0:T(8,128)(2,1)} %broadcast_in_dim.61) | data formatting | bytes 25297024 | tf_op jit(solution)/shard_map/while/body/eval_jaxpr/reshape | solution.py:25
  247.3 10.5 %slice.45 = bf16[32,197376]{1,0:T(8,128)(2,1)} slice(bf16[32,197633]{1,0:T(8,128)(2,1)} %reshape.59), slice={[0:32], [0:197376]} | slice | bytes 25264128 | tf_op jit(solution)/shard_map/while/body/eval_jaxpr/slice | solution.py:26
  257.8 12.1 %reshape.60 = bf16[32,257,768]{2,1,0:T(8,128)(2,1)} reshape(bf16[32,197376]{1,0:T(8,128)(2,1)} %slice.45) | data formatting | bytes 25264128 | tf_op jit(solution)/shard_map/while/body/eval_jaxpr/reshape | solution.py:26
  269.9 10.3 %multiply_bitcast_fusion.1 = f32[1,32,257,128]{3,2,1,0:T(8,128)} fusion(bf16[32,257,768]{2,1,0:T(8,128)(2,1)} %reshape.60, bf16[512,128]{0,1:T(8,128)(2,1)S(1)} %divide_convert_fusion), kind=kOutput, calls=%fused_computation.3 | convolution fusion | flops 1617956864 | bytes 16973824 | tf_op jit(solution)/shard_map/while/body/eval_jaxpr/alj,jr->alr/dot_general | solution.py:58
  280.2 6.4 %broadcast_in_dim.62 = bf16[32,257,769]{2,1,0:T(8,128)(2,1)} broadcast(bf16[32,769]{1,0:T(8,128)(2,1)S(1)} %pad.30), dimensions={0,2} | broadcast | bytes 12697728 | tf_op jit(solution)/shard_map/while/body/eval_jaxpr/broadcast_in_dim | solution.py:24
  286.6 15.2 %reshape.61 = bf16[32,197633]{1,0:T(8,128)(2,1)} reshape(bf16[32,257,769]{2,1,0:T(8,128)(2,1)} %broadcast_in_dim.62) | data formatting | bytes 25297024 | tf_op jit(solution)/shard_map/while/body/eval_jaxpr/reshape | solution.py:25
  301.7 10.5 %slice.46 = bf16[32,197376]{1,0:T(8,128)(2,1)} slice(bf16[32,197633]{1,0:T(8,128)(2,1)} %reshape.61), slice={[0:32], [0:197376]} | slice | bytes 25264128 | tf_op jit(solution)/shard_map/while/body/eval_jaxpr/slice | solution.py:26
  312.2 12.1 %reshape.62 = bf16[32,257,768]{2,1,0:T(8,128)(2,1)} reshape(bf16[32,197376]{1,0:T(8,128)(2,1)} %slice.46) | data formatting | bytes 25264128 | tf_op jit(solution)/shard_map/while/body/eval_jaxpr/reshape | solution.py:26
  324.3 6.7 %multiply_bitcast_fusion = f32[1,32,257,128]{3,2,1,0:T(8,128)S(1)} fusion(bf16[32,257,768]{2,1,0:T(8,128)(2,1)} %reshape.62, bf16[512,128]{0,1:T(8,128)(2,1)S(1)} %divide_convert_fusion), kind=kOutput, calls=%fused_computation.2 | convolution fusion | flops 1617956864 | bytes 16973824 | tf_op jit(solution)/shard_map/while/body/eval_jaxpr/alj,jr->alr/dot_general | solution.py:58
  331.0 8.6 %pad_maximum_fusion = f32[3,32,257,128]{3,2,1,0:T(8,128)} fusion(f32[1,32,257,128]{3,2,1,0:T(8,128)S(1)} %multiply_bitcast_fusion, f32[1,32,257,128]{3,2,1,0:T(8,128)} %multiply_bitcast_fusion.1, f32[1,32,257,128]{3,2,1,0:T(8,128)} %multiply_bitcast_fusion.2), kind=kLoop, calls=%fused_computation.1 | loop fusion | flops 6316032 | bytes 25264128 | tf_op jit(solution)/shard_map/stack | solution.py:64
  339.6 11.6 %copy.15 = f32[3,32,257,128]{3,1,2,0:T(8,128)} copy(f32[3,32,257,128]{3,2,1,0:T(8,128)} %pad_maximum_fusion) | data formatting | bytes 25264128 | tf_op jit(solution)/shard_map/stack | solution.py:64
  (1 shorter events, 0.0 us)
Async XLA Ops:
  26.6 17.5 %all-to-all-start = ((f32[16,32,128]{2,0,1:T(8,128)}), f32[16,32,128]{2,0,1:T(8,128)S(1)}, u32[]{:S(2)}, u32[]{:S(2)}) async-start(f32[16,32,128]{2,0,1:T(8,128)} %broadcast_select_fusion), calls=%async_computation | async-start | bytes 524288 | tf_op jit(solution)/shard_map/all_to_all | solution.py:32
  33.9 134.9 %all-reduce.9.cloned.1.call-start = ((), (), s32[]{:S(2)}) async-start(), calls=%async_computation.1 | async-start | bytes 196608 | tf_op jit(solution)/shard_map/psum | solution.py:18
Sparse Core Ops, SparseCore 0:
  46.6 122.1 all-reduce.8
where the time goes:
time: 360 us; the launch traced here: 358 us
  local copies, waits for them, and re-layouts  172 us (48%)
  waiting for transfers between devices  123 us (34%)
  matrix products  28.8 us (8%)
  between operations  15.3 us (4%)
  other arithmetic  11.5 us (3%)
  starting transfers between devices  7.34 us (2%)
    psum x1, waiting for transfers between devices, from_root(): return lax.psum(block, axis)  122 us
    reshape x4, local copies, waits for them, and re-layouts, shifted_rows(): flat = spread.reshape(lead + (count * period,))  47.2 us
    reshape x4, local copies, waits for them, and re-layouts, shifted_rows(): cut = flat[..., :count * (period - 1)].reshape(lead + (count, period - 1))  40 us
    slice x3, local copies, waits for them, and re-layouts, shifted_rows(): cut = flat[..., :count * (period - 1)].reshape(lead + (count, period - 1))  31.4 us
    dot_general x3, matrix products, add_block(): jnp.einsum('alj,jr->alr', hankel, window, preferred_element_type=jnp.floa...  27.2 us
    broadcast_in_dim x4, local copies, waits for them, and re-layouts, shifted_rows(): spread = jnp.broadcast_to(padded[..., None, :], lead + (count, period))  19.5 us
    gather x2, local copies, waits for them, and re-layouts, local(): columns = jnp.take(raw, chan_map, axis=1)  16.4 us
    another operation x1, local copies, waits for them, and re-layouts, local(): stacked = jnp.stack(results)  11.6 us
  transfers between devices with their start and end apart: 2, of which 2 were waited for; matrix products, arithmetic and copies ran while one was open for 2% of the time, Pallas kernels for 0%

commit v1 on v0

v1 whole, which is shorter than its diff:
```python
import functools
import math

import jax
import jax.numpy as jnp
from jax import lax
from jax.experimental import pallas as pl
from jax.experimental.pallas import tpu as pltpu
from jax.sharding import PartitionSpec as P

FIR_HALF = 64
HALF = 128
SB = 32
STEPS = 3
LAGS = 257
LANES = 128
SUB = 16
AXES = ("ch", "grp")


def regroup_kernel(order_ref, raw_ref, map_ref, out_ref, src_map):
    rows = raw_ref.shape[0]
    owners = map_ref.shape[0]
    width = src_map.shape[0]

    lane = lax.broadcasted_iota(jnp.int32, (width, LANES), 1)
    picked = jnp.zeros((width, LANES), jnp.int32)
    for step in range(STEPS):
        row = jnp.broadcast_to(map_ref[pl.ds(order_ref[step], 1), :], (width, LANES))
        if step:
            row = pltpu.roll(row, step * SB, 1)
        picked = jnp.where(lane // SB == step, row, picked)
    src_map[...] = picked

    def columns(where):
        tile = where // LANES
        spot = where % LANES
        parts = []
        for top in range(0, rows, width):
            taken = jnp.zeros((width, LANES), raw_ref.dtype)
            for block in range(owners):
                piece = raw_ref[top : top + width, block * LANES : (block + 1) * LANES]
                moved = jnp.take_along_axis(piece, spot, axis=1, mode="promise_in_bounds")
                taken = jnp.where(tile == block, moved, taken)
            parts.append(taken)
        return parts

    sources = columns(src_map[...])

    @pl.loop(0, owners)
    def _(dest):
        where = jnp.broadcast_to(map_ref[pl.ds(dest, 1), :], (width, LANES))
        own = columns(where)
        for index, top in enumerate(range(0, rows, width)):
            out_ref[dest, top : top + width, :LANES] = own[index].astype(out_ref.dtype)
            out_ref[dest, top : top + width, LANES:] = sources[index].astype(out_ref.dtype)


def regroup(raw, chan_map, order):
    rows, channels = raw.shape
    owners = channels // LANES
    return pl.pallas_call(
        regroup_kernel,
        out_shape=jax.ShapeDtypeStruct((owners, rows, 2 * LANES), jnp.float32),
        in_specs=[
            pl.BlockSpec(memory_space=pltpu.SMEM),
            pl.BlockSpec(memory_space=pltpu.VMEM),
            pl.BlockSpec(memory_space=pltpu.VMEM),
        ],
        out_specs=pl.BlockSpec(memory_space=pltpu.VMEM),
        scratch_shapes=[pltpu.VMEM((8, LANES), jnp.int32)],
        name="regroup",
    )(order, raw, chan_map.reshape(owners, LANES))


def split(value):
    high = value.astype(jnp.bfloat16)
    return high, (value - high.astype(jnp.float32)).astype(jnp.bfloat16)


def correlate_kernel(taps_ref, mixed_ref, out_ref, xh, xl, white, pair, turned, early, late, stage, sems):
    samples = mixed_ref.shape[0]

    def dot(a, b):
        return jnp.dot(a, b, preferred_element_type=jnp.float32)

    taps = jnp.broadcast_to(taps_ref[0:1, :], (LANES, 2 * LANES))
    band_h, band_l = split(pltpu.roll(taps, 0, 1, stride=1, stride_axis=0))
    edge = jnp.zeros((FIR_HALF, 2 * LANES), jnp.bfloat16)
    for ref in (xh, xl):
        ref[:FIR_HALF] = edge
        ref[FIR_HALF + samples :] = edge
    high, low = split(mixed_ref[...])
    xh[FIR_HALF : FIR_HALF + samples] = high
    xl[FIR_HALF : FIR_HALF + samples] = low
    power = jnp.zeros((1, 2 * LANES), jnp.float32)
    for start in range(0, samples, LANES):
        rows = slice(start, start + 2 * LANES)
        piece = dot(band_h, xh[rows]) + (dot(band_h, xl[rows]) + dot(band_l, xh[rows]))
        white[start : start + LANES] = piece
        power = power + jnp.sum(piece * piece, axis=0, keepdims=True)
    scale = 1.0 / jnp.sqrt(power * (1.0 / samples) + 1e-06)

    pair[...] = jnp.zeros_like(pair)
    own = (white[:, :LANES] * scale[:, :LANES]).astype(jnp.bfloat16)
    pair[HALF : HALF + samples, :LANES] = own
    pair[HALF - SUB : HALF - SUB + samples, LANES:] = own
    turned[...] = (white[:, LANES:] * scale[:, LANES:]).T

    lane = lax.broadcasted_iota(jnp.int32, (SB, samples), 1)
    gain = 1.0 / math.sqrt(samples)
    copies = []
    for step in range(STEPS):
        source = turned[step * SB : (step + 1) * SB]
        for shift in range(SUB):
            rows = slice(shift * SB, (shift + 1) * SB)
            moved = pltpu.roll(source, shift, 1) if shift else source
            late[rows] = jnp.where(lane >= shift, moved, 0.0).astype(jnp.bfloat16)
            back = SUB - shift
            moved = pltpu.roll(source, samples - back, 1)
            early[rows] = jnp.where(lane < samples - back, moved, 0.0).astype(jnp.bfloat16)
        for block in range(0, LAGS - 1, 2 * SUB):
            if block < HALF:
                part = dot(early[...], pair[block + SUB : block + SUB + samples])
            else:
                part = dot(late[...], pair[block : block + samples])
            part = part * gain
            stage[step, block : block + SUB] = part[:, :LANES].reshape(SUB, SB, LANES)
            stage[step, block + SUB : block + 2 * SUB] = part[:, LANES:].reshape(SUB, SB, LANES)
            lags = pl.ds(block, 2 * SUB)
            copies.append(pltpu.make_async_copy(stage.at[step, lags], out_ref.at[step, lags], sems.at[len(copies)]))
            copies[-1].start()
        last = dot(late[:SB], pair[2 * HALF : 2 * HALF + samples, :LANES]) * gain
        stage[step, LAGS - 1] = last
        lags = pl.ds(LAGS - 1, 1)
        copies.append(pltpu.make_async_copy(stage.at[step, lags], out_ref.at[step, lags], sems.at[len(copies)]))
        copies[-1].start()
    for copy in copies:
        copy.wait()


def correlate(fir_taps, mixed):
    samples = mixed.shape[0]
    taps = jnp.pad(fir_taps, (0, 2 * LANES - fir_taps.shape[0])).reshape(1, 2 * LANES)
    pieces = STEPS * ((LAGS - 1) // (2 * SUB) + 1)
    return pl.pallas_call(
        correlate_kernel,
        out_shape=jax.ShapeDtypeStruct((STEPS, LAGS, SB, LANES), jnp.float32),
        in_specs=[pl.BlockSpec(memory_space=pltpu.VMEM)] * 2,
        out_specs=pl.BlockSpec(memory_space=pl.ANY),
        scratch_shapes=[
            pltpu.VMEM((samples + 2 * FIR_HALF, 2 * LANES), jnp.bfloat16),
            pltpu.VMEM((samples + 2 * FIR_HALF, 2 * LANES), jnp.bfloat16),
            pltpu.VMEM((samples, 2 * LANES), jnp.float32),
            pltpu.VMEM((samples + 2 * HALF, 2 * LANES), jnp.bfloat16),
            pltpu.VMEM((LANES, samples), jnp.float32),
            pltpu.VMEM((SUB * SB, samples), jnp.bfloat16),
            pltpu.VMEM((SUB * SB, samples), jnp.bfloat16),
            pltpu.VMEM((STEPS, LAGS, SB, LANES), jnp.float32),
            pltpu.SemaphoreType.DMA((pieces,)),
        ],
        compiler_params=pltpu.CompilerParams(vmem_limit_bytes=48 * 1024 * 1024),
        name="correlate",
    )(taps, mixed)


def local(raw, fir_taps, chan_map, order):
    parts = regroup(raw, chan_map, order)
    mixed = lax.all_to_all(parts, AXES, split_axis=0, concat_axis=0, tiled=True)
    owners, rows, width = mixed.shape
    result = correlate(fir_taps, mixed.reshape(owners * rows, width))
    return jnp.transpose(result, (0, 2, 1, 3))


def solution(mesh):
    in_specs = (P(AXES, None), P(), P(), P())
    out_specs = P(None, None, None, AXES)
    return jax.shard_map(local, mesh=mesh, in_specs=in_specs, out_specs=out_specs, check_vma=False)
```

time: 360 us -> 35.4 us (0.10)
  the two profiles are of different devices: /device:TPU:0 before, /device:TPU:1 now
where the time goes in v1:
time: 35.4 us; the launch traced here: 35.2 us
  waiting for transfers between devices  14.6 us (41%)
  Pallas kernels  12.8 us (36%)
  starting transfers between devices  7.1 us (20%)
  local copies, waits for them, and re-layouts  0.68 us (2%)
    all_to_all x1, waiting for transfers between devices, local(): mixed = lax.all_to_all(parts, AXES, split_axis=0, concat_axis=0, tiled=True)  14.6 us
    all_to_all x1, starting transfers between devices, local(): mixed = lax.all_to_all(parts, AXES, split_axis=0, concat_axis=0, tiled=True)  7.1 us
    pallas_call x1, Pallas kernels, regroup(): pl.pallas_call(regroup_kernel, out_shape=jax.ShapeDtypeStruct((owners, ro...  6.65 us
    pallas_call x1, Pallas kernels, correlate(): pl.pallas_call(correlate_kernel, out_shape=jax.ShapeDtypeStruct((STEPS, L...  6.11 us
  transfers between devices with their start and end apart: 1, of which 1 were waited for; matrix products, arithmetic and copies ran while one was open for 2% of the time, Pallas kernels for 0%

profile of v1, /device:TPU:1, one launch (start us, length us, event | category | flops | bytes accessed | tf_op | source)
XLA Modules:
  0.0 35.2 jit_solution(4032699766126141037)
XLA Ops:
  0.0 6.6 %regroup.1 = f32[32,16,256]{2,1,0:T(8,128)} custom-call(s32[3]{0:T(128)} %order_ref.1, f32[16,4096]{1,0:T(8,128)} %raw_ref.1, s32[32,128]{1,0:T(8,128)} %bitcast.6), custom_call_target="tpu_custom_call" | custom-call | tf_op jit(solution)/shard_map/regroup/pallas_call | solution.py:62
  6.6 7.1 %all-to-all-start = ((f32[32,16,256]{2,1,0:T(8,128)}), f32[32,16,256]{2,1,0:T(8,128)S(1)}, u32[]{:S(2)}, u32[]{:S(2)}) async-start(f32[32,16,256]{2,1,0:T(8,128)} %regroup.1), calls=%async_computation | async-start | bytes 1048576 | tf_op jit(solution)/shard_map/all_to_all | solution.py:169
  13.8 0.7 %pad.4 = f32[256]{0:T(256)S(1)} pad(f32[129]{0:T(256)} %param.5, f32[]{:T(128)} %constant.2.clone.1), padding=0_127 | pad | bytes 1544 | tf_op jit(solution)/shard_map/jit(_pad)/pad | solution.py:144
  14.4 14.6 %all-to-all-done = f32[32,16,256]{2,1,0:T(8,128)S(1)} async-done(((f32[32,16,256]{2,1,0:T(8,128)}), f32[32,16,256]{2,1,0:T(8,128)S(1)}, u32[]{:S(2)}, u32[]{:S(2)}) %all-to-all-start) | async-done | bytes 524320 | tf_op jit(solution)/shard_map/all_to_all | solution.py:169
  29.0 6.1 %correlate.1 = f32[3,257,32,128]{3,2,1,0:T(8,128)} custom-call(f32[1,256]{1,0:T(1,128)S(1)} %bitcast.5, f32[512,256]{1,0:T(8,128)S(1)} %bitcast.4), custom_call_target="tpu_custom_call" | custom-call | tf_op jit(solution)/shard_map/correlate/pallas_call | solution.py:146
Async XLA Ops:
  6.6 22.4 %all-to-all-start = ((f32[32,16,256]{2,1,0:T(8,128)}), f32[32,16,256]{2,1,0:T(8,128)S(1)}, u32[]{:S(2)}, u32[]{:S(2)}) async-start(f32[32,16,256]{2,1,0:T(8,128)} %regroup.1), calls=%async_computation | async-start | bytes 1048576 | tf_op jit(solution)/shard_map/all_to_all | solution.py:169

commit v2 on v1

--- a/solution.py
+++ b/solution.py
@@ -15,18 +15,35 @@
 LAGS = 257
 LANES = 128
 SUB = 16
+GROUP = 4
+CODES = 32767
+OCTAVES = 32
+FLOOR = -25
 AXES = ("ch", "grp")
 
 
-def regroup_kernel(order_ref, raw_ref, map_ref, out_ref, src_map):
-    rows = raw_ref.shape[0]
+def encode(value):
+    size = jnp.maximum(jnp.abs(value), 2.0**FLOOR)
+    code = jnp.log(size) * (CODES / (OCTAVES * math.log(2.0))) + (0.5 - FLOOR * CODES / OCTAVES)
+    code = jnp.minimum(code.astype(jnp.int32), CODES)
+    return jnp.where(value < 0, -code, code)
+
+
+def decode(code):
+    size = jnp.exp(jnp.abs(code).astype(jnp.float32) * (OCTAVES * math.log(2.0) / CODES) + FLOOR * math.log(2.0))
+    size = jnp.where(code == 0, 0.0, size)
+    return jnp.where(code < 0, -size, size)
+
+
+def regroup_kernel(order_ref, raw_ref, map_ref, out_ref, packed, src_map):
+    rows = raw_ref.shape[0] // 2
     owners = map_ref.shape[0]
-    width = src_map.shape[0]
+    packed[...] = (encode(raw_ref[rows:, :]) << 16) | (encode(raw_ref[:rows, :]) & 0xFFFF)
 
-    lane = lax.broadcasted_iota(jnp.int32, (width, LANES), 1)
-    picked = jnp.zeros((width, LANES), jnp.int32)
+    lane = lax.broadcasted_iota(jnp.int32, (rows, LANES), 1)
+    picked = jnp.zeros((rows, LANES), jnp.int32)
     for step in range(STEPS):
-        row = jnp.broadcast_to(map_ref[pl.ds(order_ref[step], 1), :], (width, LANES))
+        row = jnp.broadcast_to(map_ref[pl.ds(order_ref[step], 1), :], (rows, LANES))
         if step:
             row = pltpu.roll(row, step * SB, 1)
         picked = jnp.where(lane // SB == step, row, picked)
@@ -35,25 +52,21 @@
     def columns(where):
         tile = where // LANES
         spot = where % LANES
-        parts = []
-        for top in range(0, rows, width):
-            taken = jnp.zeros((width, LANES), raw_ref.dtype)
-            for block in range(owners):
-                piece = raw_ref[top : top + width, block * LANES : (block + 1) * LANES]
-                moved = jnp.take_along_axis(piece, spot, axis=1, mode="promise_in_bounds")
-                taken = jnp.where(tile == block, moved, taken)
-            parts.append(taken)
-        return parts
+        taken = jnp.zeros((rows, LANES), jnp.int32)
+        for block in range(owners):
+            piece = packed[:, block * LANES : (block + 1) * LANES]
+            moved = jnp.take_along_axis(piece, spot, axis=1, mode="promise_in_bounds")
+            taken = jnp.where(tile == block, moved, taken)
+        return taken
 
     sources = columns(src_map[...])
 
-    @pl.loop(0, owners)
-    def _(dest):
-        where = jnp.broadcast_to(map_ref[pl.ds(dest, 1), :], (width, LANES))
-        own = columns(where)
-        for index, top in enumerate(range(0, rows, width)):
-            out_ref[dest, top : top + width, :LANES] = own[index].astype(out_ref.dtype)
-            out_ref[dest, top : top + width, LANES:] = sources[index].astype(out_ref.dtype)
+    @pl.loop(0, owners, step=GROUP)
+    def _(first):
+        for dest in range(GROUP):
+            where = jnp.broadcast_to(map_ref[pl.ds(first + dest, 1), :], (rows, LANES))
+            out_ref[first + dest, :, :LANES] = columns(where)
+            out_ref[first + dest, :, LANES:] = sources
 
 
 def regroup(raw, chan_map, order):
@@ -61,14 +74,14 @@
     owners = channels // LANES
     return pl.pallas_call(
         regroup_kernel,
-        out_shape=jax.ShapeDtypeStruct((owners, rows, 2 * LANES), jnp.float32),
+        out_shape=jax.ShapeDtypeStruct((owners, rows // 2, 2 * LANES), jnp.int32),
         in_specs=[
             pl.BlockSpec(memory_space=pltpu.SMEM),
             pl.BlockSpec(memory_space=pltpu.VMEM),
             pl.BlockSpec(memory_space=pltpu.VMEM),
         ],
         out_specs=pl.BlockSpec(memory_space=pltpu.VMEM),
-        scratch_shapes=[pltpu.VMEM((8, LANES), jnp.int32)],
+        scratch_shapes=[pltpu.VMEM((rows // 2, channels), jnp.int32), pltpu.VMEM((rows // 2, LANES), jnp.int32)],
         name="regroup",
     )(order, raw, chan_map.reshape(owners, LANES))
 
@@ -79,7 +92,8 @@
 
 
 def correlate_kernel(taps_ref, mixed_ref, out_ref, xh, xl, white, pair, turned, early, late, stage, sems):
-    samples = mixed_ref.shape[0]
+    owners, half, width = mixed_ref.shape
+    samples = owners * half * 2
 
     def dot(a, b):
         return jnp.dot(a, b, preferred_element_type=jnp.float32)
@@ -90,7 +104,9 @@
     for ref in (xh, xl):
         ref[:FIR_HALF] = edge
         ref[FIR_HALF + samples :] = edge
-    high, low = split(mixed_ref[...])
+    words = mixed_ref[...]
+    values = jnp.concatenate([decode((words << 16) >> 16), decode(words >> 16)], axis=1)
+    high, low = split(values.reshape(samples, width))
     xh[FIR_HALF : FIR_HALF + samples] = high
     xl[FIR_HALF : FIR_HALF + samples] = low
     power = jnp.zeros((1, 2 * LANES), jnp.float32)
@@ -140,7 +156,8 @@
 
 
 def correlate(fir_taps, mixed):
-    samples = mixed.shape[0]
+    owners, half, width = mixed.shape
+    samples = owners * half * 2
     taps = jnp.pad(fir_taps, (0, 2 * LANES - fir_taps.shape[0])).reshape(1, 2 * LANES)
     pieces = STEPS * ((LAGS - 1) // (2 * SUB) + 1)
     return pl.pallas_call(
@@ -167,8 +184,7 @@
 def local(raw, fir_taps, chan_map, order):
     parts = regroup(raw, chan_map, order)
     mixed = lax.all_to_all(parts, AXES, split_axis=0, concat_axis=0, tiled=True)
-    owners, rows, width = mixed.shape
-    result = correlate(fir_taps, mixed.reshape(owners * rows, width))
+    result = correlate(fir_taps, mixed)
     return jnp.transpose(result, (0, 2, 1, 3))
 
 

time: 35.4 us -> 27.6 us (0.78)
  the two profiles are of different devices: /device:TPU:1 before, /device:TPU:0 now
where the time goes in v2:
time: 27.6 us; the launch traced here: 27.4 us
  Pallas kernels  9.85 us (36%)
  waiting for transfers between devices  9.51 us (34%)
  starting transfers between devices  7.3 us (26%)
  local copies, waits for them, and re-layouts  0.68 us (2%)
    all_to_all x1, waiting for transfers between devices, local(): mixed = lax.all_to_all(parts, AXES, split_axis=0, concat_axis=0, tiled=True)  9.51 us
    all_to_all x1, starting transfers between devices, local(): mixed = lax.all_to_all(parts, AXES, split_axis=0, concat_axis=0, tiled=True)  7.3 us
    pallas_call x1, Pallas kernels, correlate(): pl.pallas_call(correlate_kernel, out_shape=jax.ShapeDtypeStruct((STEPS, L...  6.22 us
    pallas_call x1, Pallas kernels, regroup(): pl.pallas_call(regroup_kernel, out_shape=jax.ShapeDtypeStruct((owners, ro...  3.64 us
    pad x1, local copies, waits for them, and re-layouts, correlate(): jnp.pad(fir_taps, (0, 2 * LANES - fir_taps.shape[0])).reshape(1, 2 * LANES)  0.68 us
  transfers between devices with their start and end apart: 1, of which 1 were waited for; matrix products, arithmetic and copies ran while one was open for 2% of the time, Pallas kernels for 0%

profile of v2, /device:TPU:0, one launch (start us, length us, event | category | flops | bytes accessed | tf_op | source)
XLA Modules:
  0.0 27.4 jit_solution(10815739025121878940)
XLA Ops:
  0.0 3.6 %regroup.1 = s32[32,8,256]{2,1,0:T(8,128)} custom-call(s32[3]{0:T(128)} %order_ref.1, f32[16,4096]{1,0:T(8,128)} %raw_ref.1, s32[32,128]{1,0:T(8,128)} %bitcast.4), custom_call_target="tpu_custom_call" | custom-call | tf_op jit(solution)/shard_map/regroup/pallas_call | solution.py:75
  3.6 7.3 %all-to-all-start = ((s32[32,8,256]{2,1,0:T(8,128)}), s32[32,8,256]{2,1,0:T(8,128)S(1)}, u32[]{:S(2)}, u32[]{:S(2)}) async-start(s32[32,8,256]{2,1,0:T(8,128)} %regroup.1), calls=%async_computation | async-start | bytes 524288 | tf_op jit(solution)/shard_map/all_to_all | solution.py:186
  10.9 0.7 %pad.4 = f32[256]{0:T(256)S(1)} pad(f32[129]{0:T(256)} %param.5, f32[]{:T(128)} %constant.2.clone.1), padding=0_127 | pad | bytes 1544 | tf_op jit(solution)/shard_map/jit(_pad)/pad | solution.py:161
  11.6 9.5 %all-to-all-done.mixed_ref = s32[32,8,256]{2,1,0:T(8,128)S(1)} async-done(((s32[32,8,256]{2,1,0:T(8,128)}), s32[32,8,256]{2,1,0:T(8,128)S(1)}, u32[]{:S(2)}, u32[]{:S(2)}) %all-to-all-start) | async-done | bytes 262176 | tf_op jit(solution)/shard_map/all_to_all | solution.py:186
  21.1 6.2 %correlate.1 = f32[3,257,32,128]{3,2,1,0:T(8,128)} custom-call(f32[1,256]{1,0:T(1,128)S(1)} %bitcast.3, s32[32,8,256]{2,1,0:T(8,128)S(1)} %all-to-all-done.mixed_ref), custom_call_target="tpu_custom_call" | custom-call | tf_op jit(solution)/shard_map/correlate/pallas_call | solution.py:163
Async XLA Ops:
  3.6 17.5 %all-to-all-start = ((s32[32,8,256]{2,1,0:T(8,128)}), s32[32,8,256]{2,1,0:T(8,128)S(1)}, u32[]{:S(2)}, u32[]{:S(2)}) async-start(s32[32,8,256]{2,1,0:T(8,128)} %regroup.1), calls=%async_computation | async-start | bytes 524288 | tf_op jit(solution)/shard_map/all_to_all | solution.py:186

commit v3 on v2

--- a/solution.py
+++ b/solution.py
@@ -15,8 +15,10 @@
 LAGS = 257
 LANES = 128
 SUB = 16
-GROUP = 4
+GROUP = 32
 CODES = 32767
+PARTS = 4
+SENDS = ((0, 32), (32, 64), (64, 96), (96, 128), (128, 160), (160, 192), (192, 224), (224, 257))
 OCTAVES = 32
 FLOOR = -25
 AXES = ("ch", "grp")
@@ -91,7 +93,7 @@
     return high, (value - high.astype(jnp.float32)).astype(jnp.bfloat16)
 
 
-def correlate_kernel(taps_ref, mixed_ref, out_ref, xh, xl, white, pair, turned, early, late, stage, sems):
+def correlate_kernel(taps_ref, mixed_ref, out_ref, xh, xl, white, pair, turned, left, stage, sems):
     owners, half, width = mixed_ref.shape
     samples = owners * half * 2
 
@@ -121,45 +123,57 @@
     own = (white[:, :LANES] * scale[:, :LANES]).astype(jnp.bfloat16)
     pair[HALF : HALF + samples, :LANES] = own
     pair[HALF - SUB : HALF - SUB + samples, LANES:] = own
-    turned[...] = (white[:, LANES:] * scale[:, LANES:]).T
-
-    lane = lax.broadcasted_iota(jnp.int32, (SB, samples), 1)
+    turned[:, :samples] = (white[:, LANES:] * scale[:, LANES:]).T.astype(jnp.bfloat16)
+    turned[:, samples:] = jnp.zeros((LANES, LANES), jnp.bfloat16)
+
     gain = 1.0 / math.sqrt(samples)
-    copies = []
+
+    def build(step, late, shift):
+        source = turned[pl.ds(pl.multiple_of(step * SB, SB), SB), :]
+        amount = shift if late else samples + LANES - SUB + shift
+        moved = pltpu.roll(source, amount, 1) if amount else source
+        left[late, shift * SB : (shift + 1) * SB] = moved[:, :samples]
+
+    def copy(step, index):
+        start, stop = SENDS[index]
+        lags = pl.ds(start, stop - start)
+        return pltpu.make_async_copy(stage.at[step, lags], out_ref.at[step, lags], sems.at[step, index])
+
+    for shift in range(SUB):
+        build(0, 0, shift)
+    blocks = HALF // (2 * SUB)
+    deep = SUB // PARTS
+
+    @pl.loop(0, STEPS)
+    def _(step):
+        for late in range(2):
+            for index in range(blocks):
+                block = late * HALF + index * 2 * SUB
+                first = block if late else block + SUB
+                for part in range(PARTS):
+                    rows = slice(part * deep * SB, (part + 1) * deep * SB)
+                    both = dot(left[late, rows], pair[first : first + samples]) * gain
+                    low = block + part * deep
+                    stage[step, low : low + deep] = both[:, :LANES].reshape(deep, SB, LANES)
+                    stage[step, low + SUB : low + SUB + deep] = both[:, LANES:].reshape(deep, SB, LANES)
+                if block + 2 * SUB == LAGS - 1:
+                    last = dot(left[late, :SB], pair[2 * HALF : 2 * HALF + samples, :LANES])
+                    stage[step, LAGS - 1] = last * gain
+                for shift in range(index * SUB // blocks, (index + 1) * SUB // blocks):
+                    build(step + late, 1 - late, shift)
+                for piece, (_, stop) in enumerate(SENDS):
+                    if stop in (block + 2 * SUB, block + 2 * SUB + 1):
+                        copy(step, piece).start()
+
     for step in range(STEPS):
-        source = turned[step * SB : (step + 1) * SB]
-        for shift in range(SUB):
-            rows = slice(shift * SB, (shift + 1) * SB)
-            moved = pltpu.roll(source, shift, 1) if shift else source
-            late[rows] = jnp.where(lane >= shift, moved, 0.0).astype(jnp.bfloat16)
-            back = SUB - shift
-            moved = pltpu.roll(source, samples - back, 1)
-            early[rows] = jnp.where(lane < samples - back, moved, 0.0).astype(jnp.bfloat16)
-        for block in range(0, LAGS - 1, 2 * SUB):
-            if block < HALF:
-                part = dot(early[...], pair[block + SUB : block + SUB + samples])
-            else:
-                part = dot(late[...], pair[block : block + samples])
-            part = part * gain
-            stage[step, block : block + SUB] = part[:, :LANES].reshape(SUB, SB, LANES)
-            stage[step, block + SUB : block + 2 * SUB] = part[:, LANES:].reshape(SUB, SB, LANES)
-            lags = pl.ds(block, 2 * SUB)
-            copies.append(pltpu.make_async_copy(stage.at[step, lags], out_ref.at[step, lags], sems.at[len(copies)]))
-            copies[-1].start()
-        last = dot(late[:SB], pair[2 * HALF : 2 * HALF + samples, :LANES]) * gain
-        stage[step, LAGS - 1] = last
-        lags = pl.ds(LAGS - 1, 1)
-        copies.append(pltpu.make_async_copy(stage.at[step, lags], out_ref.at[step, lags], sems.at[len(copies)]))
-        copies[-1].start()
-    for copy in copies:
-        copy.wait()
+        for piece in range(len(SENDS)):
+            copy(step, piece).wait()
 
 
 def correlate(fir_taps, mixed):
     owners, half, width = mixed.shape
     samples = owners * half * 2
     taps = jnp.pad(fir_taps, (0, 2 * LANES - fir_taps.shape[0])).reshape(1, 2 * LANES)
-    pieces = STEPS * ((LAGS - 1) // (2 * SUB) + 1)
     return pl.pallas_call(
         correlate_kernel,
         out_shape=jax.ShapeDtypeStruct((STEPS, LAGS, SB, LANES), jnp.float32),
@@ -170,11 +184,10 @@
             pltpu.VMEM((samples + 2 * FIR_HALF, 2 * LANES), jnp.bfloat16),
             pltpu.VMEM((samples, 2 * LANES), jnp.float32),
             pltpu.VMEM((samples + 2 * HALF, 2 * LANES), jnp.bfloat16),
-            pltpu.VMEM((LANES, samples), jnp.float32),
-            pltpu.VMEM((SUB * SB, samples), jnp.bfloat16),
-            pltpu.VMEM((SUB * SB, samples), jnp.bfloat16),
+            pltpu.VMEM((LANES, samples + LANES), jnp.bfloat16),
+            pltpu.VMEM((2, SUB * SB, samples), jnp.bfloat16),
             pltpu.VMEM((STEPS, LAGS, SB, LANES), jnp.float32),
-            pltpu.SemaphoreType.DMA((pieces,)),
+            pltpu.SemaphoreType.DMA((STEPS, len(SENDS))),
         ],
         compiler_params=pltpu.CompilerParams(vmem_limit_bytes=48 * 1024 * 1024),
         name="correlate",

time: 27.6 us -> 26.8 us (0.971)
  Pallas kernels: 9.85 us -> 9.02 us
    pallas_call x1, Pallas kernels: 3.64 us -> 3.04 us  [regroup(): pl.pallas_call(regroup_kernel, out_shape=jax.ShapeDtypeStruct((owners, ro...]
  transfers between devices with their start and end apart: 1 -> 1, of which waited for: 1 -> 1; matrix products, arithmetic and copies ran while one was open for 2% -> 3% of each run, Pallas kernels for 0% -> 0%
where the time goes in v3:
time: 26.8 us; the launch traced here: 26.5 us
  waiting for transfers between devices  9.51 us (35%)
  Pallas kernels  9.02 us (34%)
  starting transfers between devices  7.3 us (27%)
  local copies, waits for them, and re-layouts  0.68 us (3%)
    all_to_all x1, waiting for transfers between devices, local(): mixed = lax.all_to_all(parts, AXES, split_axis=0, concat_axis=0, tiled=True)  9.51 us
    all_to_all x1, starting transfers between devices, local(): mixed = lax.all_to_all(parts, AXES, split_axis=0, concat_axis=0, tiled=True)  7.3 us
    pallas_call x1, Pallas kernels, correlate(): pl.pallas_call(correlate_kernel, out_shape=jax.ShapeDtypeStruct((STEPS, L...  5.98 us
    pallas_call x1, Pallas kernels, regroup(): pl.pallas_call(regroup_kernel, out_shape=jax.ShapeDtypeStruct((owners, ro...  3.04 us
    pad x1, local copies, waits for them, and re-layouts, correlate(): jnp.pad(fir_taps, (0, 2 * LANES - fir_taps.shape[0])).reshape(1, 2 * LANES)  0.68 us
  transfers between devices with their start and end apart: 1, of which 1 were waited for; matrix products, arithmetic and copies ran while one was open for 3% of the time, Pallas kernels for 0%

profile of v3, /device:TPU:0, one launch (start us, length us, event | category | flops | bytes accessed | tf_op | source)
XLA Modules:
  0.0 26.5 jit_solution(4823862232848240420)
XLA Ops:
  0.0 3.0 %regroup.1 = s32[32,8,256]{2,1,0:T(8,128)} custom-call(s32[3]{0:T(128)} %order_ref.1, f32[16,4096]{1,0:T(8,128)} %raw_ref.1, s32[32,128]{1,0:T(8,128)} %bitcast.4), custom_call_target="tpu_custom_call" | custom-call | tf_op jit(solution)/shard_map/regroup/pallas_call | solution.py:77
  3.0 7.3 %all-to-all-start = ((s32[32,8,256]{2,1,0:T(8,128)}), s32[32,8,256]{2,1,0:T(8,128)S(1)}, u32[]{:S(2)}, u32[]{:S(2)}) async-start(s32[32,8,256]{2,1,0:T(8,128)} %regroup.1), calls=%async_computation | async-start | bytes 524288 | tf_op jit(solution)/shard_map/all_to_all | solution.py:199
  10.3 0.7 %pad.4 = f32[256]{0:T(256)S(1)} pad(f32[129]{0:T(256)} %param.5, f32[]{:T(128)} %constant.2.clone.1), padding=0_127 | pad | bytes 1544 | tf_op jit(solution)/shard_map/jit(_pad)/pad | solution.py:176
  11.0 9.5 %all-to-all-done.mixed_ref = s32[32,8,256]{2,1,0:T(8,128)S(1)} async-done(((s32[32,8,256]{2,1,0:T(8,128)}), s32[32,8,256]{2,1,0:T(8,128)S(1)}, u32[]{:S(2)}, u32[]{:S(2)}) %all-to-all-start) | async-done | bytes 262176 | tf_op jit(solution)/shard_map/all_to_all | solution.py:199
  20.5 6.0 %correlate.1 = f32[3,257,32,128]{3,2,1,0:T(8,128)} custom-call(f32[1,256]{1,0:T(1,128)S(1)} %bitcast.3, s32[32,8,256]{2,1,0:T(8,128)S(1)} %all-to-all-done.mixed_ref), custom_call_target="tpu_custom_call" | custom-call | tf_op jit(solution)/shard_map/correlate/pallas_call | solution.py:177
Async XLA Ops:
  3.0 17.5 %all-to-all-start = ((s32[32,8,256]{2,1,0:T(8,128)}), s32[32,8,256]{2,1,0:T(8,128)S(1)}, u32[]{:S(2)}, u32[]{:S(2)}) async-start(s32[32,8,256]{2,1,0:T(8,128)} %regroup.1), calls=%async_computation | async-start | bytes 524288 | tf_op jit(solution)/shard_map/all_to_all | solution.py:199

commit v4 on v3

--- a/solution.py
+++ b/solution.py
@@ -17,6 +17,7 @@
 SUB = 16
 GROUP = 32
 CODES = 32767
+HALF_ROWS = 8
 PARTS = 4
 SENDS = ((0, 32), (32, 64), (64, 96), (96, 128), (128, 160), (160, 192), (192, 224), (224, 257))
 OCTAVES = 32
@@ -37,19 +38,20 @@
     return jnp.where(code < 0, -size, size)
 
 
-def regroup_kernel(order_ref, raw_ref, map_ref, out_ref, packed, src_map):
+def regroup_kernel(order_ref, raw_ref, map_ref, out_ref, packed):
     rows = raw_ref.shape[0] // 2
     owners = map_ref.shape[0]
+    pitch = out_ref.shape[0] // owners
     packed[...] = (encode(raw_ref[rows:, :]) << 16) | (encode(raw_ref[:rows, :]) & 0xFFFF)
 
     lane = lax.broadcasted_iota(jnp.int32, (rows, LANES), 1)
+    line = lax.broadcasted_iota(jnp.int32, (rows, LANES), 0)
     picked = jnp.zeros((rows, LANES), jnp.int32)
     for step in range(STEPS):
         row = jnp.broadcast_to(map_ref[pl.ds(order_ref[step], 1), :], (rows, LANES))
         if step:
             row = pltpu.roll(row, step * SB, 1)
         picked = jnp.where(lane // SB == step, row, picked)
-    src_map[...] = picked
 
     def columns(where):
         tile = where // LANES
@@ -61,31 +63,58 @@
             taken = jnp.where(tile == block, moved, taken)
         return taken
 
-    sources = columns(src_map[...])
+    sources = columns(picked)
+    kept = pitch - rows
+    for target in range(kept):
+        row, step = divmod(target, STEPS)
+        moved = pltpu.roll(sources, LANES - (step + 1) * SB, 1)
+        moved = jnp.broadcast_to(moved[kept + row : kept + row + 1], (rows, LANES))
+        sources = jnp.where((line == target) & (lane >= STEPS * SB), moved, sources)
 
     @pl.loop(0, owners, step=GROUP)
     def _(first):
+        start = pl.multiple_of(first * pitch, 8)
         for dest in range(GROUP):
             where = jnp.broadcast_to(map_ref[pl.ds(first + dest, 1), :], (rows, LANES))
-            out_ref[first + dest, :, :LANES] = columns(where)
-            out_ref[first + dest, :, LANES:] = sources
+            out_ref[pl.ds(start + dest * pitch, rows), :] = sources
+            out_ref[pl.ds(start + dest * pitch + kept, rows), :] = columns(where)
 
 
 def regroup(raw, chan_map, order):
     rows, channels = raw.shape
     owners = channels // LANES
+    pitch = rows // 2 * (LANES + STEPS * SB) // LANES
     return pl.pallas_call(
         regroup_kernel,
-        out_shape=jax.ShapeDtypeStruct((owners, rows // 2, 2 * LANES), jnp.int32),
+        out_shape=jax.ShapeDtypeStruct((owners * pitch, LANES), jnp.int32),
         in_specs=[
             pl.BlockSpec(memory_space=pltpu.SMEM),
             pl.BlockSpec(memory_space=pltpu.VMEM),
             pl.BlockSpec(memory_space=pltpu.VMEM),
         ],
         out_specs=pl.BlockSpec(memory_space=pltpu.VMEM),
-        scratch_shapes=[pltpu.VMEM((rows // 2, channels), jnp.int32), pltpu.VMEM((rows // 2, LANES), jnp.int32)],
+        scratch_shapes=[pltpu.VMEM((rows // 2, channels), jnp.int32)],
         name="regroup",
     )(order, raw, chan_map.reshape(owners, LANES))
+
+
+def unpack(mixed_ref, words, owners):
+    pitch = mixed_ref.shape[0] // owners
+    rows = words.shape[1] // owners
+    kept = pitch - rows
+    for owner in range(owners):
+        start = owner * pitch
+        words[0, owner * rows : (owner + 1) * rows] = mixed_ref[start + kept : start + pitch, :]
+        words[1, owner * rows : (owner + 1) * rows] = mixed_ref[start : start + rows, :]
+    lane = lax.broadcasted_iota(jnp.int32, (owners, LANES), 1)
+    for row in range(kept, rows):
+        whole = jnp.zeros((owners, LANES), jnp.int32)
+        for step in range(STEPS):
+            target = (row - kept) * STEPS + step
+            part = mixed_ref[pl.ds(target, owners, stride=pitch), :]
+            part = pltpu.roll(part, (step + 1) * SB, 1)
+            whole = jnp.where(lane // SB == step, part, whole)
+        words[1, pl.ds(row, owners, stride=rows), :] = whole
 
 
 def split(value):
@@ -93,9 +122,11 @@
     return high, (value - high.astype(jnp.float32)).astype(jnp.bfloat16)
 
 
-def correlate_kernel(taps_ref, mixed_ref, out_ref, xh, xl, white, pair, turned, left, stage, sems):
-    owners, half, width = mixed_ref.shape
-    samples = owners * half * 2
+def correlate_kernel(taps_ref, mixed_ref, out_ref, fetched, xh, xl, white, pair, turned, left, stage, sems):
+    half = fetched.shape[1]
+    owners = half // HALF_ROWS
+    samples = 2 * half
+    unpack(mixed_ref, fetched, owners)
 
     def dot(a, b):
         return jnp.dot(a, b, preferred_element_type=jnp.float32)
@@ -106,9 +137,9 @@
     for ref in (xh, xl):
         ref[:FIR_HALF] = edge
         ref[FIR_HALF + samples :] = edge
-    words = mixed_ref[...]
+    words = jnp.concatenate([fetched[0], fetched[1]], axis=1).reshape(owners, HALF_ROWS, 2 * LANES)
     values = jnp.concatenate([decode((words << 16) >> 16), decode(words >> 16)], axis=1)
-    high, low = split(values.reshape(samples, width))
+    high, low = split(values.reshape(samples, 2 * LANES))
     xh[FIR_HALF : FIR_HALF + samples] = high
     xl[FIR_HALF : FIR_HALF + samples] = low
     power = jnp.zeros((1, 2 * LANES), jnp.float32)
@@ -129,7 +160,7 @@
     gain = 1.0 / math.sqrt(samples)
 
     def build(step, late, shift):
-        source = turned[pl.ds(pl.multiple_of(step * SB, SB), SB), :]
+        source = turned[pl.ds(step * SB, SB), :]
         amount = shift if late else samples + LANES - SUB + shift
         moved = pltpu.roll(source, amount, 1) if amount else source
         left[late, shift * SB : (shift + 1) * SB] = moved[:, :samples]
@@ -144,8 +175,7 @@
     blocks = HALF // (2 * SUB)
     deep = SUB // PARTS
 
-    @pl.loop(0, STEPS)
-    def _(step):
+    for step in range(STEPS):
         for late in range(2):
             for index in range(blocks):
                 block = late * HALF + index * 2 * SUB
@@ -170,9 +200,7 @@
             copy(step, piece).wait()
 
 
-def correlate(fir_taps, mixed):
-    owners, half, width = mixed.shape
-    samples = owners * half * 2
+def correlate(fir_taps, mixed, samples):
     taps = jnp.pad(fir_taps, (0, 2 * LANES - fir_taps.shape[0])).reshape(1, 2 * LANES)
     return pl.pallas_call(
         correlate_kernel,
@@ -180,6 +208,7 @@
         in_specs=[pl.BlockSpec(memory_space=pltpu.VMEM)] * 2,
         out_specs=pl.BlockSpec(memory_space=pl.ANY),
         scratch_shapes=[
+            pltpu.VMEM((2, samples // 2, LANES), jnp.int32),
             pltpu.VMEM((samples + 2 * FIR_HALF, 2 * LANES), jnp.bfloat16),
             pltpu.VMEM((samples + 2 * FIR_HALF, 2 * LANES), jnp.bfloat16),
             pltpu.VMEM((samples, 2 * LANES), jnp.float32),
@@ -196,8 +225,11 @@
 
 def local(raw, fir_taps, chan_map, order):
     parts = regroup(raw, chan_map, order)
+    rows, channels = raw.shape
+    owners = channels // LANES
+    parts = parts.reshape(owners, -1, 1, LANES)
     mixed = lax.all_to_all(parts, AXES, split_axis=0, concat_axis=0, tiled=True)
-    result = correlate(fir_taps, mixed)
+    result = correlate(fir_taps, mixed.reshape(-1, LANES), owners * rows)
     return jnp.transpose(result, (0, 2, 1, 3))
 
 

time: 26.8 us -> 26.2 us (0.978)
  waiting for transfers between devices: 9.51 us -> 9.11 us
    all_to_all x1, waiting for transfers between devices: 9.51 us -> 9.11 us  [local(): mixed = lax.all_to_all(parts, AXES, split_axis=0, concat_axis=0, tiled=True)]
where the time goes in v4:
time: 26.2 us; the launch traced here: 26 us
  waiting for transfers between devices  9.11 us (35%)
  Pallas kernels  8.89 us (34%)
  starting transfers between devices  7.3 us (28%)
  local copies, waits for them, and re-layouts  0.68 us (3%)
    all_to_all x1, waiting for transfers between devices, local(): mixed = lax.all_to_all(parts, AXES, split_axis=0, concat_axis=0, tiled=True)  9.11 us
    all_to_all x1, starting transfers between devices, local(): mixed = lax.all_to_all(parts, AXES, split_axis=0, concat_axis=0, tiled=True)  7.3 us
    pallas_call x1, Pallas kernels, correlate(): pl.pallas_call(correlate_kernel, out_shape=jax.ShapeDtypeStruct((STEPS, L...  5.85 us
    pallas_call x1, Pallas kernels, regroup(): pl.pallas_call(regroup_kernel, out_shape=jax.ShapeDtypeStruct((owners * p...  3.04 us
    pad x1, local copies, waits for them, and re-layouts, correlate(): jnp.pad(fir_taps, (0, 2 * LANES - fir_taps.shape[0])).reshape(1, 2 * LANES)  0.68 us
  transfers between devices with their start and end apart: 1, of which 1 were waited for; matrix products, arithmetic and copies ran while one was open for 3% of the time, Pallas kernels for 0%

profile of v4, /device:TPU:0, one launch (start us, length us, event | category | flops | bytes accessed | tf_op | source)
XLA Modules:
  0.0 26.0 jit_solution(11339874065098332630)
XLA Ops:
  0.0 3.0 %regroup.1 = s32[448,128]{1,0:T(8,128)} custom-call(s32[3]{0:T(128)} %order_ref.1, f32[16,4096]{1,0:T(8,128)} %raw_ref.1, s32[32,128]{1,0:T(8,128)} %bitcast.8), custom_call_target="tpu_custom_call" | custom-call | tf_op jit(solution)/shard_map/regroup/pallas_call | solution.py:87
  3.0 7.3 %all-to-all-start = ((s32[32,14,1,128]{3,2,1,0:T(1,128)}), s32[32,14,1,128]{3,2,1,0:T(1,128)S(1)}, u32[]{:S(2)}, u32[]{:S(2)}) async-start(s32[32,14,1,128]{3,2,1,0:T(1,128)} %bitcast.7), calls=%async_computation | async-start | bytes 458752 | tf_op jit(solution)/shard_map/all_to_all | solution.py:231
  10.3 0.7 %pad.4 = f32[256]{0:T(256)S(1)} pad(f32[129]{0:T(256)} %param.5, f32[]{:T(128)} %constant.2.clone.1), padding=0_127 | pad | bytes 1544 | tf_op jit(solution)/shard_map/jit(_pad)/pad | solution.py:204
  11.0 9.1 %all-to-all-done = s32[32,14,1,128]{3,2,1,0:T(1,128)S(1)} async-done(((s32[32,14,1,128]{3,2,1,0:T(1,128)}), s32[32,14,1,128]{3,2,1,0:T(1,128)S(1)}, u32[]{:S(2)}, u32[]{:S(2)}) %all-to-all-start) | async-done | bytes 229408 | tf_op jit(solution)/shard_map/all_to_all | solution.py:231
  20.1 5.8 %correlate.1 = f32[3,257,32,128]{3,2,1,0:T(8,128)} custom-call(f32[1,256]{1,0:T(1,128)S(1)} %bitcast.6, s32[448,128]{1,0:T(8,128)S(1)} %bitcast.5), custom_call_target="tpu_custom_call" | custom-call | tf_op jit(solution)/shard_map/correlate/pallas_call | solution.py:205
Async XLA Ops:
  3.0 17.1 %all-to-all-start = ((s32[32,14,1,128]{3,2,1,0:T(1,128)}), s32[32,14,1,128]{3,2,1,0:T(1,128)S(1)}, u32[]{:S(2)}, u32[]{:S(2)}) async-start(s32[32,14,1,128]{3,2,1,0:T(1,128)} %bitcast.7), calls=%async_computation | async-start | bytes 458752 | tf_op jit(solution)/shard_map/all_to_all | solution.py:231

commit v5 on v4

--- a/solution.py
+++ b/solution.py
@@ -133,6 +133,7 @@
 
     taps = jnp.broadcast_to(taps_ref[0:1, :], (LANES, 2 * LANES))
     band_h, band_l = split(pltpu.roll(taps, 0, 1, stride=1, stride_axis=0))
+    band = jnp.concatenate([band_h, band_l, band_h], axis=1)
     edge = jnp.zeros((FIR_HALF, 2 * LANES), jnp.bfloat16)
     for ref in (xh, xl):
         ref[:FIR_HALF] = edge
@@ -145,16 +146,20 @@
     power = jnp.zeros((1, 2 * LANES), jnp.float32)
     for start in range(0, samples, LANES):
         rows = slice(start, start + 2 * LANES)
-        piece = dot(band_h, xh[rows]) + (dot(band_h, xl[rows]) + dot(band_l, xh[rows]))
+        piece = dot(band, jnp.concatenate([xl[rows], xh[rows], xh[rows]], axis=0))
         white[start : start + LANES] = piece
         power = power + jnp.sum(piece * piece, axis=0, keepdims=True)
     scale = 1.0 / jnp.sqrt(power * (1.0 / samples) + 1e-06)
 
-    pair[...] = jnp.zeros_like(pair)
+    for top in range(0, HALF, SUB):
+        gap = jnp.zeros((SUB, 2 * LANES), jnp.bfloat16)
+        pair[top : top + SUB] = gap
+        pair[samples + HALF - SUB + top : samples + HALF + top] = gap
+    pair[samples + 2 * HALF - SUB :] = jnp.zeros((SUB, 2 * LANES), jnp.bfloat16)
     own = (white[:, :LANES] * scale[:, :LANES]).astype(jnp.bfloat16)
     pair[HALF : HALF + samples, :LANES] = own
     pair[HALF - SUB : HALF - SUB + samples, LANES:] = own
-    turned[:, :samples] = (white[:, LANES:] * scale[:, LANES:]).T.astype(jnp.bfloat16)
+    turned[:, :samples] = (white[:, LANES:] * scale[:, LANES:]).astype(jnp.bfloat16).T
     turned[:, samples:] = jnp.zeros((LANES, LANES), jnp.bfloat16)
 
     gain = 1.0 / math.sqrt(samples)
@@ -167,11 +172,9 @@
 
     def copy(step, index):
         start, stop = SENDS[index]
-        lags = pl.ds(start, stop - start)
-        return pltpu.make_async_copy(stage.at[step, lags], out_ref.at[step, lags], sems.at[step, index])
-
-    for shift in range(SUB):
-        build(0, 0, shift)
+        rows = pl.ds((step * LAGS + start) * SB, (stop - start) * SB)
+        return pltpu.make_async_copy(stage.at[rows, :], out_ref.at[rows, :], sems.at[step, index])
+
     blocks = HALF // (2 * SUB)
     deep = SUB // PARTS
 
@@ -181,14 +184,19 @@
                 block = late * HALF + index * 2 * SUB
                 first = block if late else block + SUB
                 for part in range(PARTS):
+                    if step == late == index == 0:
+                        for shift in range(part * deep, (part + 1) * deep):
+                            build(0, 0, shift)
                     rows = slice(part * deep * SB, (part + 1) * deep * SB)
                     both = dot(left[late, rows], pair[first : first + samples]) * gain
                     low = block + part * deep
-                    stage[step, low : low + deep] = both[:, :LANES].reshape(deep, SB, LANES)
-                    stage[step, low + SUB : low + SUB + deep] = both[:, LANES:].reshape(deep, SB, LANES)
+                    top = (step * LAGS + low) * SB
+                    stage[top : top + deep * SB] = both[:, :LANES]
+                    stage[top + SUB * SB : top + (SUB + deep) * SB] = both[:, LANES:]
                 if block + 2 * SUB == LAGS - 1:
                     last = dot(left[late, :SB], pair[2 * HALF : 2 * HALF + samples, :LANES])
-                    stage[step, LAGS - 1] = last * gain
+                    top = (step * LAGS + LAGS - 1) * SB
+                    stage[top : top + SB] = last * gain
                 for shift in range(index * SUB // blocks, (index + 1) * SUB // blocks):
                     build(step + late, 1 - late, shift)
                 for piece, (_, stop) in enumerate(SENDS):
@@ -204,7 +212,7 @@
     taps = jnp.pad(fir_taps, (0, 2 * LANES - fir_taps.shape[0])).reshape(1, 2 * LANES)
     return pl.pallas_call(
         correlate_kernel,
-        out_shape=jax.ShapeDtypeStruct((STEPS, LAGS, SB, LANES), jnp.float32),
+        out_shape=jax.ShapeDtypeStruct((STEPS * LAGS * SB, LANES), jnp.float32),
         in_specs=[pl.BlockSpec(memory_space=pltpu.VMEM)] * 2,
         out_specs=pl.BlockSpec(memory_space=pl.ANY),
         scratch_shapes=[
@@ -215,7 +223,7 @@
             pltpu.VMEM((samples + 2 * HALF, 2 * LANES), jnp.bfloat16),
             pltpu.VMEM((LANES, samples + LANES), jnp.bfloat16),
             pltpu.VMEM((2, SUB * SB, samples), jnp.bfloat16),
-            pltpu.VMEM((STEPS, LAGS, SB, LANES), jnp.float32),
+            pltpu.VMEM((STEPS * LAGS * SB, LANES), jnp.float32),
             pltpu.SemaphoreType.DMA((STEPS, len(SENDS))),
         ],
         compiler_params=pltpu.CompilerParams(vmem_limit_bytes=48 * 1024 * 1024),
@@ -230,7 +238,7 @@
     parts = parts.reshape(owners, -1, 1, LANES)
     mixed = lax.all_to_all(parts, AXES, split_axis=0, concat_axis=0, tiled=True)
     result = correlate(fir_taps, mixed.reshape(-1, LANES), owners * rows)
-    return jnp.transpose(result, (0, 2, 1, 3))
+    return jnp.transpose(result.reshape(STEPS, LAGS, SB, LANES), (0, 2, 1, 3))
 
 
 def solution(mesh):

time: 26.2 us -> 26.3 us (level)
  no operation moved by 1% of the time
where the time goes in v5:
time: 26.3 us; the launch traced here: 26 us
  waiting for transfers between devices  9.11 us (35%)
  Pallas kernels  8.9 us (34%)
  starting transfers between devices  7.3 us (28%)
  local copies, waits for them, and re-layouts  0.68 us (3%)
    all_to_all x1, waiting for transfers between devices, local(): mixed = lax.all_to_all(parts, AXES, split_axis=0, concat_axis=0, tiled=True)  9.11 us
    all_to_all x1, starting transfers between devices, local(): mixed = lax.all_to_all(parts, AXES, split_axis=0, concat_axis=0, tiled=True)  7.3 us
    pallas_call x1, Pallas kernels, correlate(): pl.pallas_call(correlate_kernel, out_shape=jax.ShapeDtypeStruct((STEPS *...  5.86 us
    pallas_call x1, Pallas kernels, regroup(): pl.pallas_call(regroup_kernel, out_shape=jax.ShapeDtypeStruct((owners * p...  3.04 us
    pad x1, local copies, waits for them, and re-layouts, correlate(): jnp.pad(fir_taps, (0, 2 * LANES - fir_taps.shape[0])).reshape(1, 2 * LANES)  0.68 us
  transfers between devices with their start and end apart: 1, of which 1 were waited for; matrix products, arithmetic and copies ran while one was open for 3% of the time, Pallas kernels for 0%

profile of v5, /device:TPU:0, one launch (start us, length us, event | category | flops | bytes accessed | tf_op | source)
XLA Modules:
  0.0 26.0 jit_solution(14738279502457189763)
XLA Ops:
  0.0 3.0 %regroup.1 = s32[448,128]{1,0:T(8,128)} custom-call(s32[3]{0:T(128)} %order_ref.1, f32[16,4096]{1,0:T(8,128)} %raw_ref.1, s32[32,128]{1,0:T(8,128)} %bitcast.10), custom_call_target="tpu_custom_call" | custom-call | tf_op jit(solution)/shard_map/regroup/pallas_call | solution.py:87
  3.0 7.3 %all-to-all-start = ((s32[32,14,1,128]{3,2,1,0:T(1,128)}), s32[32,14,1,128]{3,2,1,0:T(1,128)S(1)}, u32[]{:S(2)}, u32[]{:S(2)}) async-start(s32[32,14,1,128]{3,2,1,0:T(1,128)} %bitcast.9), calls=%async_computation | async-start | bytes 458752 | tf_op jit(solution)/shard_map/all_to_all | solution.py:239
  10.3 0.7 %pad.4 = f32[256]{0:T(256)S(1)} pad(f32[129]{0:T(256)} %param.5, f32[]{:T(128)} %constant.2.clone.1), padding=0_127 | pad | bytes 1544 | tf_op jit(solution)/shard_map/jit(_pad)/pad | solution.py:212
  11.0 9.1 %all-to-all-done = s32[32,14,1,128]{3,2,1,0:T(1,128)S(1)} async-done(((s32[32,14,1,128]{3,2,1,0:T(1,128)}), s32[32,14,1,128]{3,2,1,0:T(1,128)S(1)}, u32[]{:S(2)}, u32[]{:S(2)}) %all-to-all-start) | async-done | bytes 229408 | tf_op jit(solution)/shard_map/all_to_all | solution.py:239
  20.1 5.9 %correlate.1 = f32[24672,128]{1,0:T(8,128)} custom-call(f32[1,256]{1,0:T(1,128)S(1)} %bitcast.8, s32[448,128]{1,0:T(8,128)S(1)} %bitcast.7), custom_call_target="tpu_custom_call" | custom-call | tf_op jit(solution)/shard_map/correlate/pallas_call | solution.py:213
Async XLA Ops:
  3.0 17.1 %all-to-all-start = ((s32[32,14,1,128]{3,2,1,0:T(1,128)}), s32[32,14,1,128]{3,2,1,0:T(1,128)S(1)}, u32[]{:S(2)}, u32[]{:S(2)}) async-start(s32[32,14,1,128]{3,2,1,0:T(1,128)} %bitcast.9), calls=%async_computation | async-start | bytes 458752 | tf_op jit(solution)/shard_map/all_to_all | solution.py:239

commit v6 on v5

--- a/solution.py
+++ b/solution.py
@@ -193,10 +193,11 @@
                     top = (step * LAGS + low) * SB
                     stage[top : top + deep * SB] = both[:, :LANES]
                     stage[top + SUB * SB : top + (SUB + deep) * SB] = both[:, LANES:]
-                if block + 2 * SUB == LAGS - 1:
-                    last = dot(left[late, :SB], pair[2 * HALF : 2 * HALF + samples, :LANES])
-                    top = (step * LAGS + LAGS - 1) * SB
-                    stage[top : top + SB] = last * gain
+                if step == late == index == 0:
+                    last = dot(turned[: STEPS * SB, :samples], pair[2 * HALF : 2 * HALF + samples, :LANES]) * gain
+                    for each in range(STEPS):
+                        top = (each * LAGS + LAGS - 1) * SB
+                        stage[top : top + SB] = last[each * SB : (each + 1) * SB]
                 for shift in range(index * SUB // blocks, (index + 1) * SUB // blocks):
                     build(step + late, 1 - late, shift)
                 for piece, (_, stop) in enumerate(SENDS):

time: 26.3 us -> 26.3 us (level)
  no operation moved by 1% of the time
where the time goes in v6:
time: 26.3 us; the launch traced here: 26 us
  waiting for transfers between devices  9.11 us (35%)
  Pallas kernels  8.94 us (34%)
  starting transfers between devices  7.3 us (28%)
  local copies, waits for them, and re-layouts  0.68 us (3%)
    all_to_all x1, waiting for transfers between devices, local(): mixed = lax.all_to_all(parts, AXES, split_axis=0, concat_axis=0, tiled=True)  9.11 us
    all_to_all x1, starting transfers between devices, local(): mixed = lax.all_to_all(parts, AXES, split_axis=0, concat_axis=0, tiled=True)  7.3 us
    pallas_call x1, Pallas kernels, correlate(): pl.pallas_call(correlate_kernel, out_shape=jax.ShapeDtypeStruct((STEPS *...  5.89 us
    pallas_call x1, Pallas kernels, regroup(): pl.pallas_call(regroup_kernel, out_shape=jax.ShapeDtypeStruct((owners * p...  3.04 us
    pad x1, local copies, waits for them, and re-layouts, correlate(): jnp.pad(fir_taps, (0, 2 * LANES - fir_taps.shape[0])).reshape(1, 2 * LANES)  0.68 us
  transfers between devices with their start and end apart: 1, of which 1 were waited for; matrix products, arithmetic and copies ran while one was open for 3% of the time, Pallas kernels for 0%

profile of v6, /device:TPU:0, one launch (start us, length us, event | category | flops | bytes accessed | tf_op | source)
XLA Modules:
  0.0 26.0 jit_solution(8405370499193909214)
XLA Ops:
  0.0 3.0 %regroup.1 = s32[448,128]{1,0:T(8,128)} custom-call(s32[3]{0:T(128)} %order_ref.1, f32[16,4096]{1,0:T(8,128)} %raw_ref.1, s32[32,128]{1,0:T(8,128)} %bitcast.10), custom_call_target="tpu_custom_call" | custom-call | tf_op jit(solution)/shard_map/regroup/pallas_call | solution.py:87
  3.0 7.3 %all-to-all-start = ((s32[32,14,1,128]{3,2,1,0:T(1,128)}), s32[32,14,1,128]{3,2,1,0:T(1,128)S(1)}, u32[]{:S(2)}, u32[]{:S(2)}) async-start(s32[32,14,1,128]{3,2,1,0:T(1,128)} %bitcast.9), calls=%async_computation | async-start | bytes 458752 | tf_op jit(solution)/shard_map/all_to_all | solution.py:240
  10.3 0.7 %pad.4 = f32[256]{0:T(256)S(1)} pad(f32[129]{0:T(256)} %param.5, f32[]{:T(128)} %constant.2.clone.1), padding=0_127 | pad | bytes 1544 | tf_op jit(solution)/shard_map/jit(_pad)/pad | solution.py:213
  11.0 9.1 %all-to-all-done = s32[32,14,1,128]{3,2,1,0:T(1,128)S(1)} async-done(((s32[32,14,1,128]{3,2,1,0:T(1,128)}), s32[32,14,1,128]{3,2,1,0:T(1,128)S(1)}, u32[]{:S(2)}, u32[]{:S(2)}) %all-to-all-start) | async-done | bytes 229408 | tf_op jit(solution)/shard_map/all_to_all | solution.py:240
  20.1 5.9 %correlate.1 = f32[24672,128]{1,0:T(8,128)} custom-call(f32[1,256]{1,0:T(1,128)S(1)} %bitcast.8, s32[448,128]{1,0:T(8,128)S(1)} %bitcast.7), custom_call_target="tpu_custom_call" | custom-call | tf_op jit(solution)/shard_map/correlate/pallas_call | solution.py:214
Async XLA Ops:
  3.0 17.1 %all-to-all-start = ((s32[32,14,1,128]{3,2,1,0:T(1,128)}), s32[32,14,1,128]{3,2,1,0:T(1,128)S(1)}, u32[]{:S(2)}, u32[]{:S(2)}) async-start(s32[32,14,1,128]{3,2,1,0:T(1,128)} %bitcast.9), calls=%async_computation | async-start | bytes 458752 | tf_op jit(solution)/shard_map/all_to_all | solution.py:240
